TPU v7x, 256 devices: a whole 4x4x8 slice. The times are simulated.
256 devices in a mesh: grp: 8 (over x, y_hi), blk: 32 (over z, y_lo, core).
Axes of the slice: x: 4, y: 4 (y_hi: 2, y_lo: 2; y = y_hi * 2 + y_lo), z: 8, core: 2. Of those that a mesh axis runs over, the one named last changes fastest.
Arguments:
- counts: int32 [65536, 1024], P(('grp', 'blk')), may hold values from 0 to 5
- tile_live: int32 [512, 8], P(('grp', 'blk')), may hold values from 0 to 1
- doc_lengths: int32 [65536], P(('grp', 'blk')), may hold values from 256 to 4095
- doc_mix: bfloat16 [65536, 4096], P(('grp', 'blk')), may hold values from 0.019897461 to 50
- word_topic: float32 [4096, 4096], P('blk'), may hold values from 0.01 to 8
- topic_total: float32 [4096], replicated, may hold values from 20000 to 400000
Outputs:
- doc_share: bfloat16 [65536, 4096], P(('grp', 'blk'))
- word_topic_new: float32 [4096, 4096], P('blk')
- topic_mean: float32 [4096], replicated
All inputs are finite; a program needn't handle non-finite values.
Results may differ from a plain program's by a relative error of at most 0.0004.
The roundings to bfloat16 on the way count: a program that leaves them out, or rounds other values in their place, can miss the bound.
Values may be sent and summed in bfloat16 or wider, within the bound.
A program may use at most 128 MiB of HBM per device.

v0:
```python
import jax
import jax.numpy as jnp
from jax import lax
from jax.sharding import PartitionSpec as P

VOCAB = 262144
alpha_prior = 0.1
beta_prior = 0.01


def passed_along(block, axis, distance):
    devices = range(lax.axis_size(axis))
    route = [((i - distance) % len(devices), i) for i in devices]
    return lax.ppermute(block, axis, route)


def tile_terms(operands):
    doc_rows, block_counts, visitor = operands
    normalizer = jnp.dot(doc_rows, visitor.T, preferred_element_type=jnp.float32)
    ratio = (block_counts / normalizer).astype(jnp.bfloat16)
    doc_part = jnp.dot(ratio, visitor, preferred_element_type=jnp.float32)
    word_part = jnp.dot(ratio.T, doc_rows, preferred_element_type=jnp.float32)
    return (doc_part, word_part)


def shard_terms(visitor, block_counts, doc_low):
    return tile_terms((doc_low, block_counts, visitor))


def local(counts, tile_live, doc_lengths, doc_mix, word_topic, topic_total):
    block_rows = word_topic.shape[0]
    visits = tile_live.shape[1]
    word_weight = (word_topic + beta_prior) / (topic_total + beta_prior * VOCAB)[None, :]
    word_low = word_weight.astype(jnp.bfloat16)
    mix_wide = doc_mix.astype(jnp.float32)
    doc_theta = mix_wide / jnp.sum(mix_wide, axis=1, keepdims=True)
    doc_weight = doc_lengths.astype(jnp.float32)[:, None] * doc_theta + alpha_prior
    doc_low = doc_weight.astype(jnp.bfloat16)
    live_full = jnp.repeat(jnp.repeat(tile_live, block_rows, axis=0), block_rows, axis=1)
    live_counts = counts.astype(jnp.float32) * live_full.astype(jnp.float32)
    window_len = jnp.sum(live_counts, axis=1)
    doc_proj = jnp.zeros((doc_low.shape[0], doc_low.shape[1]), jnp.float32)
    word_accum = jnp.zeros((block_rows, doc_low.shape[1]), jnp.float32)
    visitor = word_low
    for offset in range(visits):
        if offset > 0:
            visitor, word_accum = (
                passed_along(visitor.astype(jnp.float32), "blk", -1).astype(visitor.dtype),
                passed_along(word_accum, "blk", -1),
            )
        block_counts = live_counts[:, offset * block_rows : (offset + 1) * block_rows]
        doc_part, word_part = shard_terms(visitor, block_counts, doc_low)
        doc_proj = doc_proj + doc_part
        word_accum = word_accum + word_part
    word_accum = passed_along(word_accum, "blk", visits - 1)
    doc_new = doc_weight * doc_proj
    column_sum = jnp.sum(doc_new, axis=0)
    topic_count = doc_low.shape[1]
    doc_share = (
        topic_count * (doc_new + alpha_prior) / (window_len[:, None] + topic_count * alpha_prior)
    ).astype(jnp.bfloat16)
    word_sum = lax.psum(word_accum, "grp")
    topic_sum = lax.psum(column_sum, ("grp", "blk"))
    vocab_window = block_rows * lax.axis_size("blk")
    return (doc_share, word_weight * word_sum, topic_sum / vocab_window)


def solution(mesh):
    return jax.shard_map(
        local,
        mesh=mesh,
        in_specs=(
            P(("grp", "blk"), None),
            P(("grp", "blk"), None),
            P(("grp", "blk")),
            P(("grp", "blk"), None),
            P("blk", None),
            P(),
        ),
        out_specs=(P(("grp", "blk"), None), P("blk", None), P()),
        check_vma=False,
    )
```

profile of v0, /device:TPU:161, one launch (start us, length us, event | category | flops | bytes accessed | tf_op | source)
XLA Modules:
  0.0 519.2 jit_solution(7656554678656352072)
XLA Ops:
  7.2 0.8 convert_element_type.95
  8.1 2.0 convert_reduce_fusion
  10.0 0.7 broadcast_add_fusion
  10.7 1.0 fusion.8
  12.4 1.0 copy-done
  13.7 0.7 fusion.9
  14.8 0.8 collective-permute-start.7
  15.6 1.5 collective-permute-start
  17.1 34.7 %collective-permute-done = bf16[128,4096]{1,0:T(8,128)(2,1)S(1)} collective-permute-done((bf16[128,4096]{1,0:T(8,128)(2,1)S(1)}, bf16[128,4096]{1,0:T(8,128)(2,1)S(1)}, u32[]{:S(2)}, u32[]{:S(2)}) %collective-permute-start) | collective-permute-done | bytes 1048608 | tf_op jit(solution)/shard_map/ppermute | solution.py:14
  51.7 0.7 fusion.10
  52.5 0.5 convolution_add_fusion.2
  53.2 2.8 collective-permute-start.1
  56.0 33.8 %collective-permute-done.1 = bf16[128,4096]{1,0:T(8,128)(2,1)S(1)} collective-permute-done((bf16[128,4096]{1,0:T(8,128)(2,1)S(1)}, bf16[128,4096]{1,0:T(8,128)(2,1)S(1)}, u32[]{:S(2)}, u32[]{:S(2)}) %collective-permute-start.1) | collective-permute-done | bytes 1048608 | tf_op jit(solution)/shard_map/ppermute | solution.py:14
  89.8 0.7 fusion.11
  90.5 0.5 fusion.42
  91.3 1.1 collective-permute-start.9
  92.4 2.8 collective-permute-start.2
  95.2 32.9 %collective-permute-done.2 = bf16[128,4096]{1,0:T(8,128)(2,1)S(1)} collective-permute-done((bf16[128,4096]{1,0:T(8,128)(2,1)S(1)}, bf16[128,4096]{1,0:T(8,128)(2,1)S(1)}, u32[]{:S(2)}, u32[]{:S(2)}) %collective-permute-start.2) | collective-permute-done | bytes 1048608 | tf_op jit(solution)/shard_map/ppermute | solution.py:14
  128.0 0.7 fusion.12
  129.5 2.0 collective-permute-start.10
  131.5 2.8 collective-permute-start.3
  134.3 32.0 %collective-permute-done.3 = bf16[128,4096]{1,0:T(8,128)(2,1)S(1)} collective-permute-done((bf16[128,4096]{1,0:T(8,128)(2,1)S(1)}, bf16[128,4096]{1,0:T(8,128)(2,1)S(1)}, u32[]{:S(2)}, u32[]{:S(2)}) %collective-permute-start.3) | collective-permute-done | bytes 1048608 | tf_op jit(solution)/shard_map/ppermute | solution.py:14
  166.3 0.7 fusion.13
  167.7 2.9 collective-permute-start.11
  170.6 2.8 collective-permute-start.4
  173.4 31.1 %collective-permute-done.4 = bf16[128,4096]{1,0:T(8,128)(2,1)S(1)} collective-permute-done((bf16[128,4096]{1,0:T(8,128)(2,1)S(1)}, bf16[128,4096]{1,0:T(8,128)(2,1)S(1)}, u32[]{:S(2)}, u32[]{:S(2)}) %collective-permute-start.4) | collective-permute-done | bytes 1048608 | tf_op jit(solution)/shard_map/ppermute | solution.py:14
  204.5 0.7 fusion.14
  206.0 3.8 collective-permute-start.12
  209.8 2.8 collective-permute-start.5
  212.6 30.2 %collective-permute-done.5 = bf16[128,4096]{1,0:T(8,128)(2,1)S(1)} collective-permute-done((bf16[128,4096]{1,0:T(8,128)(2,1)S(1)}, bf16[128,4096]{1,0:T(8,128)(2,1)S(1)}, u32[]{:S(2)}, u32[]{:S(2)}) %collective-permute-start.5) | collective-permute-done | bytes 1048608 | tf_op jit(solution)/shard_map/ppermute | solution.py:14
  242.7 0.7 fusion.15
  244.2 4.7 collective-permute-start.13
  248.9 2.8 collective-permute-start.6
  251.7 0.7 fusion.40
  252.4 28.6 %collective-permute-done.6 = bf16[128,4096]{1,0:T(8,128)(2,1)S(1)} collective-permute-done((bf16[128,4096]{1,0:T(8,128)(2,1)S(1)}, bf16[128,4096]{1,0:T(8,128)(2,1)S(1)}, u32[]{:S(2)}, u32[]{:S(2)}) %collective-permute-start.6) | collective-permute-done | bytes 1048608 | tf_op jit(solution)/shard_map/ppermute | solution.py:14
  281.0 0.7 fusion.16
  282.4 6.9 %collective-permute-start.14 = (f32[128,4096]{1,0:T(8,128)S(1)}, f32[128,4096]{1,0:T(8,128)}, u32[]{:S(2)}, u32[]{:S(2)}) collective-permute-start(f32[128,4096]{1,0:T(8,128)S(1)} %add.96), channel_id=1, source_target_pairs={{25,0},{26,1},{27,2},{28,3},{29,4},{30,5},{31,6},{0,7},{1,8},{2,9}... | collective-permute-start | bytes 6291464 | tf_op jit(solution)/shard_map/ppermute | solution.py:14
  289.3 2.7 convolution_add_fusion.1
  292.0 2.6 fusion.52
  294.6 2.6 fusion.51
  297.2 2.7 fusion.50
  299.9 2.7 fusion.49
  302.6 2.6 fusion.48
  305.2 69.0 %collective-permute-done.14 = f32[128,4096]{1,0:T(8,128)} collective-permute-done((f32[128,4096]{1,0:T(8,128)S(1)}, f32[128,4096]{1,0:T(8,128)}, u32[]{:S(2)}, u32[]{:S(2)}) %collective-permute-start.14) | collective-permute-done | bytes 2097184 | tf_op jit(solution)/shard_map/ppermute | solution.py:14
  374.2 11.5 %fusion.39 = (f32[4096]{0:T(1024)S(1)}, bf16[256,4096]{1,0:T(8,128)(2,1)}) fusion(f32[256]{0:T(256)S(1)} %broadcast_add_fusion.1, f32[256,4096]{1,0:T(8,128)} %fusion.48, f32[256,4096]{1,0:T(8,128)} %fusion.49, f32[256,4096]{1,0:T(8,128)} %fusion.50, f32[256,4096]{1,0:T(8,128)} %fusion.51, f32[256,4096]{1,0:T(8,128)} %fusion.52, ...), kind=kOutput, calls=%fused_computation.64 | convolution fusion | flops 285208576 | bytes 30493696 | tf_op jit(solution)/shard_map/dot_general | solution.py:21
  385.7 122.8 %psum.15 = f32[4096]{0:T(1024)S(1)} all-reduce(f32[4096]{0:T(1024)S(1)} %get-tuple-element.5), channel_id=1, replica_groups=mesh['grp'=8,'blk'=32] {'grp','blk'}, use_global_device_ids=true, to_apply=%region_4.0 | all-reduce | flops 4096 | bytes 32768 | tf_op jit(solution)/shard_map/psum | solution.py:63
  508.5 0.6 broadcast_multiply_fusion
  509.1 3.2 fusion.17
  (36 shorter events, 5.5 us)
Async XLA Ops:
  7.2 3.6 copy-start.1
  7.2 2.8 copy-start.3
  7.2 501.9 %all-reduce.2.cloned.1.call-start = ((), (), s32[]{:S(2)}) async-start(), calls=%async_computation | async-start | bytes 4194304 | tf_op jit(solution)/shard_map/psum | solution.py:62
  10.7 1.4 copy-start.2
  11.8 1.6 copy-start
  14.8 37.6 %collective-permute-start.7 = (f32[128,4096]{1,0:T(8,128)S(1)}, f32[128,4096]{1,0:T(8,128)S(1)}, u32[]{:S(2)}, u32[]{:S(2)}) collective-permute-start(f32[128,4096]{1,0:T(8,128)S(1)} %fusion.41), channel_id=1, source_target_pairs={{1,0},{2,1},{3,2},{4,3},{5,4},{6,5},{7,6},{8,7},{9,8},{10,9},{11,1... | collective-permute-start | bytes 6291464 | tf_op jit(solution)/shard_map/ppermute | solution.py:14
  15.6 36.1 %collective-permute-start = (bf16[128,4096]{1,0:T(8,128)(2,1)S(1)}, bf16[128,4096]{1,0:T(8,128)(2,1)S(1)}, u32[]{:S(2)}, u32[]{:S(2)}) collective-permute-start(bf16[128,4096]{1,0:T(8,128)(2,1)S(1)} %fusion.18), channel_id=1, source_target_pairs={{1,0},{2,1},{3,2},{4,3},{5,4},{6,5},{7,6},{8,7},{9,8},{10,9},{11,1... | collective-permute-start | bytes 3145736 | tf_op jit(solution)/shard_map/ppermute | solution.py:14
  53.0 38.0 %collective-permute-start.8 = (f32[128,4096]{1,0:T(8,128)S(1)}, f32[128,4096]{1,0:T(8,128)S(1)}, u32[]{:S(2)}, u32[]{:S(2)}) collective-permute-start(f32[128,4096]{1,0:T(8,128)S(1)} %convolution_add_fusion.2), channel_id=1, source_target_pairs={{1,0},{2,1},{3,2},{4,3},{5,4},{6,5},{7,6},{8,7},{9,8},{10,9},{11,1... | collective-permute-start | bytes 6291464 | tf_op jit(solution)/shard_map/ppermute | solution.py:14
  53.2 36.6 %collective-permute-start.1 = (bf16[128,4096]{1,0:T(8,128)(2,1)S(1)}, bf16[128,4096]{1,0:T(8,128)(2,1)S(1)}, u32[]{:S(2)}, u32[]{:S(2)}) collective-permute-start(bf16[128,4096]{1,0:T(8,128)(2,1)S(1)} %collective-permute-done), channel_id=1, source_target_pairs={{1,0},{2,1},{3,2},{4,3},{5,4},{6,5},{7,6},{8,7},{9,8},{10,9},{11,1... | collective-permute-start | bytes 3145736 | tf_op jit(solution)/shard_map/ppermute | solution.py:14
  91.3 38.0 %collective-permute-start.9 = (f32[128,4096]{1,0:T(8,128)S(1)}, f32[128,4096]{1,0:T(8,128)S(1)}, u32[]{:S(2)}, u32[]{:S(2)}) collective-permute-start(f32[128,4096]{1,0:T(8,128)S(1)} %add.91), channel_id=1, source_target_pairs={{1,0},{2,1},{3,2},{4,3},{5,4},{6,5},{7,6},{8,7},{9,8},{10,9},{11,1... | collective-permute-start | bytes 6291464 | tf_op jit(solution)/shard_map/ppermute | solution.py:14
  92.4 35.7 %collective-permute-start.2 = (bf16[128,4096]{1,0:T(8,128)(2,1)S(1)}, bf16[128,4096]{1,0:T(8,128)(2,1)S(1)}, u32[]{:S(2)}, u32[]{:S(2)}) collective-permute-start(bf16[128,4096]{1,0:T(8,128)(2,1)S(1)} %collective-permute-done.1), channel_id=1, source_target_pairs={{1,0},{2,1},{3,2},{4,3},{5,4},{6,5},{7,6},{8,7},{9,8},{10,9},{11,1... | collective-permute-start | bytes 3145736 | tf_op jit(solution)/shard_map/ppermute | solution.py:14
  129.5 38.0 %collective-permute-start.10 = (f32[128,4096]{1,0:T(8,128)S(1)}, f32[128,4096]{1,0:T(8,128)S(1)}, u32[]{:S(2)}, u32[]{:S(2)}) collective-permute-start(f32[128,4096]{1,0:T(8,128)S(1)} %add.92), channel_id=1, source_target_pairs={{1,0},{2,1},{3,2},{4,3},{5,4},{6,5},{7,6},{8,7},{9,8},{10,9},{11,1... | collective-permute-start | bytes 6291464 | tf_op jit(solution)/shard_map/ppermute | solution.py:14
  131.5 34.8 %collective-permute-start.3 = (bf16[128,4096]{1,0:T(8,128)(2,1)S(1)}, bf16[128,4096]{1,0:T(8,128)(2,1)S(1)}, u32[]{:S(2)}, u32[]{:S(2)}) collective-permute-start(bf16[128,4096]{1,0:T(8,128)(2,1)S(1)} %collective-permute-done.2), channel_id=1, source_target_pairs={{1,0},{2,1},{3,2},{4,3},{5,4},{6,5},{7,6},{8,7},{9,8},{10,9},{11,1... | collective-permute-start | bytes 3145736 | tf_op jit(solution)/shard_map/ppermute | solution.py:14
  167.7 38.0 %collective-permute-start.11 = (f32[128,4096]{1,0:T(8,128)S(1)}, f32[128,4096]{1,0:T(8,128)S(1)}, u32[]{:S(2)}, u32[]{:S(2)}) collective-permute-start(f32[128,4096]{1,0:T(8,128)S(1)} %add.93), channel_id=1, source_target_pairs={{1,0},{2,1},{3,2},{4,3},{5,4},{6,5},{7,6},{8,7},{9,8},{10,9},{11,1... | collective-permute-start | bytes 6291464 | tf_op jit(solution)/shard_map/ppermute | solution.py:14
  170.6 33.9 %collective-permute-start.4 = (bf16[128,4096]{1,0:T(8,128)(2,1)S(1)}, bf16[128,4096]{1,0:T(8,128)(2,1)S(1)}, u32[]{:S(2)}, u32[]{:S(2)}) collective-permute-start(bf16[128,4096]{1,0:T(8,128)(2,1)S(1)} %collective-permute-done.3), channel_id=1, source_target_pairs={{1,0},{2,1},{3,2},{4,3},{5,4},{6,5},{7,6},{8,7},{9,8},{10,9},{11,1... | collective-permute-start | bytes 3145736 | tf_op jit(solution)/shard_map/ppermute | solution.py:14
  206.0 38.0 %collective-permute-start.12 = (f32[128,4096]{1,0:T(8,128)S(1)}, f32[128,4096]{1,0:T(8,128)S(1)}, u32[]{:S(2)}, u32[]{:S(2)}) collective-permute-start(f32[128,4096]{1,0:T(8,128)S(1)} %add.94), channel_id=1, source_target_pairs={{1,0},{2,1},{3,2},{4,3},{5,4},{6,5},{7,6},{8,7},{9,8},{10,9},{11,1... | collective-permute-start | bytes 6291464 | tf_op jit(solution)/shard_map/ppermute | solution.py:14
  209.8 33.0 %collective-permute-start.5 = (bf16[128,4096]{1,0:T(8,128)(2,1)S(1)}, bf16[128,4096]{1,0:T(8,128)(2,1)S(1)}, u32[]{:S(2)}, u32[]{:S(2)}) collective-permute-start(bf16[128,4096]{1,0:T(8,128)(2,1)S(1)} %collective-permute-done.4), channel_id=1, source_target_pairs={{1,0},{2,1},{3,2},{4,3},{5,4},{6,5},{7,6},{8,7},{9,8},{10,9},{11,1... | collective-permute-start | bytes 3145736 | tf_op jit(solution)/shard_map/ppermute | solution.py:14
  244.2 38.0 %collective-permute-start.13 = (f32[128,4096]{1,0:T(8,128)S(1)}, f32[128,4096]{1,0:T(8,128)S(1)}, u32[]{:S(2)}, u32[]{:S(2)}) collective-permute-start(f32[128,4096]{1,0:T(8,128)S(1)} %add.95), channel_id=1, source_target_pairs={{1,0},{2,1},{3,2},{4,3},{5,4},{6,5},{7,6},{8,7},{9,8},{10,9},{11,1... | collective-permute-start | bytes 6291464 | tf_op jit(solution)/shard_map/ppermute | solution.py:14
  248.9 32.1 %collective-permute-start.6 = (bf16[128,4096]{1,0:T(8,128)(2,1)S(1)}, bf16[128,4096]{1,0:T(8,128)(2,1)S(1)}, u32[]{:S(2)}, u32[]{:S(2)}) collective-permute-start(bf16[128,4096]{1,0:T(8,128)(2,1)S(1)} %collective-permute-done.5), channel_id=1, source_target_pairs={{1,0},{2,1},{3,2},{4,3},{5,4},{6,5},{7,6},{8,7},{9,8},{10,9},{11,1... | collective-permute-start | bytes 3145736 | tf_op jit(solution)/shard_map/ppermute | solution.py:14
  282.4 91.8 %collective-permute-start.14 = (f32[128,4096]{1,0:T(8,128)S(1)}, f32[128,4096]{1,0:T(8,128)}, u32[]{:S(2)}, u32[]{:S(2)}) collective-permute-start(f32[128,4096]{1,0:T(8,128)S(1)} %add.96), channel_id=1, source_target_pairs={{25,0},{26,1},{27,2},{28,3},{29,4},{30,5},{31,6},{0,7},{1,8},{2,9}... | collective-permute-start | bytes 6291464 | tf_op jit(solution)/shard_map/ppermute | solution.py:14
Sparse Core Ops, SparseCore 0:
  374.3 117.2 all-reduce.1
where the time goes:
time: 520 us; the launch traced here: 519 us
  waiting for transfers between devices  292 us (56%)
  blocking collectives  123 us (24%)
  starting transfers between devices  40.6 us (8%)
  matrix products  37.6 us (7%)
  between operations  14.3 us (3%)
  other arithmetic  10.4 us (2%)
    ppermute x15, waiting for transfers between devices, passed_along(): return lax.ppermute(block, axis, route)  292 us
    psum x1, blocking collectives, local(): topic_sum = lax.psum(column_sum, ('grp', 'blk'))  123 us
    ppermute x15, starting transfers between devices, passed_along(): return lax.ppermute(block, axis, route)  40.6 us
    dot_general x8, matrix products, tile_terms(): doc_part = jnp.dot(ratio, visitor, preferred_element_type=jnp.float32)  28.1 us
  transfers between devices with their start and end apart: 16, of which 8 were waited for; matrix products, arithmetic and copies ran while one was open for 7% of the time, Pallas kernels for 0%

commit v1 on v0

--- a/solution.py
+++ b/solution.py
@@ -1,3 +1,4 @@
+import functools
 import jax
 import jax.numpy as jnp
 from jax import lax
@@ -6,6 +7,13 @@
 VOCAB = 262144
 alpha_prior = 0.1
 beta_prior = 0.01
+
+
+def begin_pages(x0, which_axis):
+    return lax.all_gather(x0, which_axis).sum(axis=0)
+
+
+cubes_take = functools.partial(begin_pages, which_axis=("grp", "blk"))
 
 
 def passed_along(block, axis, distance):
@@ -60,7 +68,7 @@
         topic_count * (doc_new + alpha_prior) / (window_len[:, None] + topic_count * alpha_prior)
     ).astype(jnp.bfloat16)
     word_sum = lax.psum(word_accum, "grp")
-    topic_sum = lax.psum(column_sum, ("grp", "blk"))
+    topic_sum = cubes_take(column_sum)
     vocab_window = block_rows * lax.axis_size("blk")
     return (doc_share, word_weight * word_sum, topic_sum / vocab_window)
 

time: 520 us -> 769 us (1.48); the launches traced: 519 us -> 760 us
  waiting for transfers between devices: 292 us -> 663 us
  blocking collectives: 123 us -> 0 us
  matrix products: 37.6 us -> 27.9 us
  starting transfers between devices: 40.6 us -> 32.4 us
    all_gather x0 -> x1, waiting for transfers between devices: none -> 390 us  [begin_pages(): return lax.all_gather(x0, which_axis).sum(axis=0)]
    psum x1 -> x0, blocking collectives: 123 us -> none  [local(): topic_sum = lax.psum(column_sum, ('grp', 'blk'))]
    ppermute x15, waiting for transfers between devices: 292 us -> 272 us  [passed_along(): return lax.ppermute(block, axis, route)]
    dot_general x8, matrix products: 28.1 us -> 17.4 us  [tile_terms(): doc_part = jnp.dot(ratio, visitor, preferred_element_type=jnp.float32)]
    ppermute x15, starting transfers between devices: 40.6 us -> 32.3 us  [passed_along(): return lax.ppermute(block, axis, route)]
  transfers between devices with their start and end apart: 16 -> 17, of which waited for: 8 -> 13; matrix products, arithmetic and copies ran while one was open for 7% -> 5% of each run, Pallas kernels for 0% -> 0%
where the time goes in v1:
time: 769 us; the launch traced here: 760 us
  waiting for transfers between devices  663 us (86%)
  starting transfers between devices  32.4 us (4%)
  matrix products  27.9 us (4%)
  between operations  15.8 us (2%)
  other arithmetic  15.3 us (2%)
    all_gather x1, waiting for transfers between devices, begin_pages(): return lax.all_gather(x0, which_axis).sum(axis=0)  390 us
    ppermute x15, waiting for transfers between devices, passed_along(): return lax.ppermute(block, axis, route)  272 us
    ppermute x15, starting transfers between devices, passed_along(): return lax.ppermute(block, axis, route)  32.3 us
    dot_general x8, matrix products, tile_terms(): doc_part = jnp.dot(ratio, visitor, preferred_element_type=jnp.float32)  17.4 us
  transfers between devices with their start and end apart: 17, of which 13 were waited for; matrix products, arithmetic and copies ran while one was open for 5% of the time, Pallas kernels for 0%

profile of v1, /device:TPU:161, one launch (start us, length us, event | category | flops | bytes accessed | tf_op | source)
XLA Modules:
  0.0 760.1 jit_solution(70079653835055854)
XLA Ops:
  8.1 0.9 broadcast_add_fusion
  8.9 2.0 fusion.18
  10.9 0.8 collective-permute-start
  12.1 1.0 fusion.8
  13.7 0.7 fusion.9
  15.0 1.5 collective-permute-start.7
  16.5 8.9 %collective-permute-done = bf16[128,4096]{1,0:T(8,128)(2,1)S(1)} collective-permute-done((bf16[128,4096]{1,0:T(8,128)(2,1)S(1)}, bf16[128,4096]{1,0:T(8,128)(2,1)S(1)}, u32[]{:S(2)}, u32[]{:S(2)}) %collective-permute-start) | collective-permute-done | bytes 1048608 | tf_op jit(solution)/shard_map/ppermute | solution.py:22
  25.4 0.7 fusion.10
  26.2 32.9 %collective-permute-done.1 = bf16[128,4096]{1,0:T(8,128)(2,1)S(1)} collective-permute-done((bf16[128,4096]{1,0:T(8,128)(2,1)S(1)}, bf16[128,4096]{1,0:T(8,128)(2,1)S(1)}, u32[]{:S(2)}, u32[]{:S(2)}) %collective-permute-start.1) | collective-permute-done | bytes 1048608 | tf_op jit(solution)/shard_map/ppermute | solution.py:22
  59.7 2.9 collective-permute-start.8
  62.6 10.7 %collective-permute-done.2 = bf16[128,4096]{1,0:T(8,128)(2,1)S(1)} collective-permute-done((bf16[128,4096]{1,0:T(8,128)(2,1)S(1)}, bf16[128,4096]{1,0:T(8,128)(2,1)S(1)}, u32[]{:S(2)}, u32[]{:S(2)}) %collective-permute-start.2) | collective-permute-done | bytes 1048608 | tf_op jit(solution)/shard_map/ppermute | solution.py:22
  73.3 1.0 collective-permute-start.3
  74.3 0.7 fusion.40
  75.0 0.7 fusion.11
  76.4 19.4 %collective-permute-done.8 = f32[128,4096]{1,0:T(8,128)S(1)} collective-permute-done((f32[128,4096]{1,0:T(8,128)S(1)}, f32[128,4096]{1,0:T(8,128)S(1)}, u32[]{:S(2)}, u32[]{:S(2)}) %collective-permute-start.8) | collective-permute-done | bytes 2097184 | tf_op jit(solution)/shard_map/ppermute | solution.py:22
  96.0 1.1 collective-permute-start.9
  97.1 9.9 %collective-permute-done.3 = bf16[128,4096]{1,0:T(8,128)(2,1)S(1)} collective-permute-done((bf16[128,4096]{1,0:T(8,128)(2,1)S(1)}, bf16[128,4096]{1,0:T(8,128)(2,1)S(1)}, u32[]{:S(2)}, u32[]{:S(2)}) %collective-permute-start.3) | collective-permute-done | bytes 1048608 | tf_op jit(solution)/shard_map/ppermute | solution.py:22
  107.0 1.0 collective-permute-start.4
  108.7 0.7 fusion.12
  110.1 30.6 %collective-permute-done.4 = bf16[128,4096]{1,0:T(8,128)(2,1)S(1)} collective-permute-done((bf16[128,4096]{1,0:T(8,128)(2,1)S(1)}, bf16[128,4096]{1,0:T(8,128)(2,1)S(1)}, u32[]{:S(2)}, u32[]{:S(2)}) %collective-permute-start.4) | collective-permute-done | bytes 1048608 | tf_op jit(solution)/shard_map/ppermute | solution.py:22
  140.7 1.0 collective-permute-start.5
  142.2 0.7 fusion.13
  142.9 0.7 fusion.51
  143.9 2.9 collective-permute-start.10
  147.2 7.7 %collective-permute-done.5 = bf16[128,4096]{1,0:T(8,128)(2,1)S(1)} collective-permute-done((bf16[128,4096]{1,0:T(8,128)(2,1)S(1)}, bf16[128,4096]{1,0:T(8,128)(2,1)S(1)}, u32[]{:S(2)}, u32[]{:S(2)}) %collective-permute-start.5) | collective-permute-done | bytes 1048608 | tf_op jit(solution)/shard_map/ppermute | solution.py:22
  154.9 1.9 collective-permute-start.6
  156.8 0.7 fusion.14
  158.9 0.7 fusion.15
  159.6 2.6 fusion.49
  162.3 26.3 %collective-permute-done.6 = bf16[128,4096]{1,0:T(8,128)(2,1)S(1)} collective-permute-done((bf16[128,4096]{1,0:T(8,128)(2,1)S(1)}, bf16[128,4096]{1,0:T(8,128)(2,1)S(1)}, u32[]{:S(2)}, u32[]{:S(2)}) %collective-permute-start.6) | collective-permute-done | bytes 1048608 | tf_op jit(solution)/shard_map/ppermute | solution.py:22
  188.6 0.7 fusion.16
  189.4 2.7 fusion.48
  192.1 1.5 add.91
  193.6 1.9 collective-permute-start.11
  195.5 8.6 %fusion.39 = (f32[4096]{0:T(1024)}, bf16[256,4096]{1,0:T(8,128)(2,1)}) fusion(f32[256]{0:T(256)S(1)} %broadcast_add_fusion.1, f32[256,4096]{1,0:T(8,128)} %fusion.48, f32[256,4096]{1,0:T(8,128)} %fusion.49, f32[256,4096]{1,0:T(8,128)S(1)} %fusion.50, f32[256,4096]{1,0:T(8,128)S(1)} %fusion.51, f32[256,4096]{1,0:T(8,128)S(1)} %fusion.52, ...), kind=kOutput, calls=%fused_computation.64 | convolution fusion | flops 285208576 | bytes 30493696 | tf_op jit(solution)/shard_map/dot_general | solution.py:29
  204.2 1.3 fusion.45
  205.5 13.9 %collective-permute-done.11 = f32[128,4096]{1,0:T(8,128)} collective-permute-done((f32[128,4096]{1,0:T(8,128)}, f32[128,4096]{1,0:T(8,128)}, u32[]{:S(2)}, u32[]{:S(2)}) %collective-permute-start.11) | collective-permute-done | bytes 2097184 | tf_op jit(solution)/shard_map/ppermute | solution.py:22
  219.4 1.9 add.92
  221.2 2.9 collective-permute-start.12
  224.6 22.2 %collective-permute-done.12 = f32[128,4096]{1,0:T(8,128)S(1)} collective-permute-done((f32[128,4096]{1,0:T(8,128)S(1)}, f32[128,4096]{1,0:T(8,128)S(1)}, u32[]{:S(2)}, u32[]{:S(2)}) %collective-permute-start.12) | collective-permute-done | bytes 2097184 | tf_op jit(solution)/shard_map/ppermute | solution.py:22
  247.0 5.2 collective-permute-start.13
  252.7 19.8 %collective-permute-done.13 = f32[128,4096]{1,0:T(8,128)S(1)} collective-permute-done((f32[128,4096]{1,0:T(8,128)S(1)}, f32[128,4096]{1,0:T(8,128)S(1)}, u32[]{:S(2)}, u32[]{:S(2)}) %collective-permute-start.13) | collective-permute-done | bytes 2097184 | tf_op jit(solution)/shard_map/ppermute | solution.py:22
  272.8 7.9 %collective-permute-start.14 = (f32[128,4096]{1,0:T(8,128)S(1)}, f32[128,4096]{1,0:T(8,128)}, u32[]{:S(2)}, u32[]{:S(2)}) collective-permute-start(f32[128,4096]{1,0:T(8,128)S(1)} %add.94), channel_id=1, source_target_pairs={{25,0},{26,1},{27,2},{28,3},{29,4},{30,5},{31,6},{0,7},{1,8},{2,9}... | collective-permute-start | bytes 6291464 | tf_op jit(solution)/shard_map/ppermute | solution.py:22
  280.7 70.1 %collective-permute-done.14 = f32[128,4096]{1,0:T(8,128)} collective-permute-done((f32[128,4096]{1,0:T(8,128)S(1)}, f32[128,4096]{1,0:T(8,128)}, u32[]{:S(2)}, u32[]{:S(2)}) %collective-permute-start.14) | collective-permute-done | bytes 2097184 | tf_op jit(solution)/shard_map/ppermute | solution.py:22
  350.9 390.4 %all-gather.3.cloned.1.call-done = f32[1048576]{0:T(1024)} async-done(((f32[4096]{0:T(1024)}), f32[1048576]{0:T(1024)}) %all-gather.3.cloned.1.call-update) | async-done | bytes 4194320 | tf_op jit(solution)/shard_map/all_gather | solution.py:13
  741.2 5.0 reshape.17
  746.2 2.5 reduce_sum.39
  749.4 3.3 fusion.17
  (58 shorter events, 9.2 us)
Async XLA Ops:
  8.0 3.7 copy-start.10
  8.0 3.7 copy-start.1
  8.0 733.2 %all-gather.3.cloned.1.call-start = ((), (), s32[]{:S(2)}) async-start(), calls=%async_computation.1 | async-start | bytes 4210688 | tf_op jit(solution)/shard_map/all_gather | solution.py:13
  8.9 3.1 copy-start.11
  8.9 3.1 copy-start.2
  10.9 14.4 %collective-permute-start = (bf16[128,4096]{1,0:T(8,128)(2,1)S(1)}, bf16[128,4096]{1,0:T(8,128)(2,1)S(1)}, u32[]{:S(2)}, u32[]{:S(2)}) collective-permute-start(bf16[128,4096]{1,0:T(8,128)(2,1)S(1)} %fusion.18), channel_id=1, source_target_pairs={{1,0},{2,1},{3,2},{4,3},{5,4},{6,5},{7,6},{8,7},{9,8},{10,9},{11,1... | collective-permute-start | bytes 3145736 | tf_op jit(solution)/shard_map/ppermute | solution.py:22
  12.1 1.4 copy-start.3
  15.0 44.2 %collective-permute-start.7 = (f32[128,4096]{1,0:T(8,128)S(1)}, f32[128,4096]{1,0:T(8,128)S(1)}, u32[]{:S(2)}, u32[]{:S(2)}) collective-permute-start(f32[128,4096]{1,0:T(8,128)S(1)} %fusion.41), channel_id=1, source_target_pairs={{1,0},{2,1},{3,2},{4,3},{5,4},{6,5},{7,6},{8,7},{9,8},{10,9},{11,1... | collective-permute-start | bytes 6291464 | tf_op jit(solution)/shard_map/ppermute | solution.py:22
  25.3 33.7 %collective-permute-start.1 = (bf16[128,4096]{1,0:T(8,128)(2,1)S(1)}, bf16[128,4096]{1,0:T(8,128)(2,1)S(1)}, u32[]{:S(2)}, u32[]{:S(2)}) collective-permute-start(bf16[128,4096]{1,0:T(8,128)(2,1)S(1)} %collective-permute-done), channel_id=1, source_target_pairs={{1,0},{2,1},{3,2},{4,3},{5,4},{6,5},{7,6},{8,7},{9,8},{10,9},{11,1... | collective-permute-start | bytes 3145736 | tf_op jit(solution)/shard_map/ppermute | solution.py:22
  59.0 15.9 %copy-start.12 = (bf16[128,4096]{1,0:T(8,128)(2,1)}, bf16[128,4096]{1,0:T(8,128)(2,1)S(1)}, u32[]{:S(2)}) copy-start(bf16[128,4096]{1,0:T(8,128)(2,1)S(1)} %collective-permute-done.1) | copy-start | bytes 3145732
  59.0 14.2 %collective-permute-start.2 = (bf16[128,4096]{1,0:T(8,128)(2,1)S(1)}, bf16[128,4096]{1,0:T(8,128)(2,1)S(1)}, u32[]{:S(2)}, u32[]{:S(2)}) collective-permute-start(bf16[128,4096]{1,0:T(8,128)(2,1)S(1)} %collective-permute-done.1), channel_id=1, source_target_pairs={{1,0},{2,1},{3,2},{4,3},{5,4},{6,5},{7,6},{8,7},{9,8},{10,9},{11,1... | collective-permute-start | bytes 3145736 | tf_op jit(solution)/shard_map/ppermute | solution.py:22
  59.7 36.1 %collective-permute-start.8 = (f32[128,4096]{1,0:T(8,128)S(1)}, f32[128,4096]{1,0:T(8,128)S(1)}, u32[]{:S(2)}, u32[]{:S(2)}) collective-permute-start(f32[128,4096]{1,0:T(8,128)S(1)} %convolution_add_fusion.2), channel_id=1, source_target_pairs={{1,0},{2,1},{3,2},{4,3},{5,4},{6,5},{7,6},{8,7},{9,8},{10,9},{11,1... | collective-permute-start | bytes 6291464 | tf_op jit(solution)/shard_map/ppermute | solution.py:22
  73.3 33.7 %collective-permute-start.3 = (bf16[128,4096]{1,0:T(8,128)(2,1)S(1)}, bf16[128,4096]{1,0:T(8,128)(2,1)S(1)}, u32[]{:S(2)}, u32[]{:S(2)}) collective-permute-start(bf16[128,4096]{1,0:T(8,128)(2,1)S(1)} %collective-permute-done.2), channel_id=1, source_target_pairs={{1,0},{2,1},{3,2},{4,3},{5,4},{6,5},{7,6},{8,7},{9,8},{10,9},{11,1... | collective-permute-start | bytes 3145736 | tf_op jit(solution)/shard_map/ppermute | solution.py:22
  75.7 0.6 copy-start.9
  96.0 47.6 %collective-permute-start.9 = (f32[128,4096]{1,0:T(8,128)S(1)}, f32[128,4096]{1,0:T(8,128)S(1)}, u32[]{:S(2)}, u32[]{:S(2)}) collective-permute-start(f32[128,4096]{1,0:T(8,128)S(1)} %add.89), channel_id=1, source_target_pairs={{1,0},{2,1},{3,2},{4,3},{5,4},{6,5},{7,6},{8,7},{9,8},{10,9},{11,1... | collective-permute-start | bytes 6291464 | tf_op jit(solution)/shard_map/ppermute | solution.py:22
  107.0 33.7 %collective-permute-start.4 = (bf16[128,4096]{1,0:T(8,128)(2,1)S(1)}, bf16[128,4096]{1,0:T(8,128)(2,1)S(1)}, u32[]{:S(2)}, u32[]{:S(2)}) collective-permute-start(bf16[128,4096]{1,0:T(8,128)(2,1)S(1)} %collective-permute-done.3), channel_id=1, source_target_pairs={{1,0},{2,1},{3,2},{4,3},{5,4},{6,5},{7,6},{8,7},{9,8},{10,9},{11,1... | collective-permute-start | bytes 3145736 | tf_op jit(solution)/shard_map/ppermute | solution.py:22
  140.7 14.2 %collective-permute-start.5 = (bf16[128,4096]{1,0:T(8,128)(2,1)S(1)}, bf16[128,4096]{1,0:T(8,128)(2,1)S(1)}, u32[]{:S(2)}, u32[]{:S(2)}) collective-permute-start(bf16[128,4096]{1,0:T(8,128)(2,1)S(1)} %collective-permute-done.4), channel_id=1, source_target_pairs={{1,0},{2,1},{3,2},{4,3},{5,4},{6,5},{7,6},{8,7},{9,8},{10,9},{11,1... | collective-permute-start | bytes 3145736 | tf_op jit(solution)/shard_map/ppermute | solution.py:22
  143.9 48.2 %collective-permute-start.10 = (f32[128,4096]{1,0:T(8,128)S(1)}, f32[128,4096]{1,0:T(8,128)S(1)}, u32[]{:S(2)}, u32[]{:S(2)}) collective-permute-start(f32[128,4096]{1,0:T(8,128)S(1)} %add.90), channel_id=1, source_target_pairs={{1,0},{2,1},{3,2},{4,3},{5,4},{6,5},{7,6},{8,7},{9,8},{10,9},{11,1... | collective-permute-start | bytes 6291464 | tf_op jit(solution)/shard_map/ppermute | solution.py:22
  154.9 33.7 %collective-permute-start.6 = (bf16[128,4096]{1,0:T(8,128)(2,1)S(1)}, bf16[128,4096]{1,0:T(8,128)(2,1)S(1)}, u32[]{:S(2)}, u32[]{:S(2)}) collective-permute-start(bf16[128,4096]{1,0:T(8,128)(2,1)S(1)} %collective-permute-done.5), channel_id=1, source_target_pairs={{1,0},{2,1},{3,2},{4,3},{5,4},{6,5},{7,6},{8,7},{9,8},{10,9},{11,1... | collective-permute-start | bytes 3145736 | tf_op jit(solution)/shard_map/ppermute | solution.py:22
  157.6 0.6 copy-start.8
  159.6 2.7 copy-start.6
  189.3 2.7 copy-start.4
  193.6 25.8 %collective-permute-start.11 = (f32[128,4096]{1,0:T(8,128)}, f32[128,4096]{1,0:T(8,128)}, u32[]{:S(2)}, u32[]{:S(2)}) collective-permute-start(f32[128,4096]{1,0:T(8,128)} %add.91), channel_id=1, source_target_pairs={{1,0},{2,1},{3,2},{4,3},{5,4},{6,5},{7,6},{8,7},{9,8},{10,9},{11,1... | collective-permute-start | bytes 6291464 | tf_op jit(solution)/shard_map/ppermute | solution.py:22
  204.1 545.3 %all-reduce.2.cloned.1.call-start = ((), (), s32[]{:S(2)}) async-start(), calls=%async_computation | async-start | bytes 4194304 | tf_op jit(solution)/shard_map/psum | solution.py:70
  205.5 18.6 %copy-start.7 = (bf16[256,128]{1,0:T(8,128)(2,1)S(1)}, bf16[256,128]{1,0:T(8,128)(2,1)}, u32[]{:S(2)}) copy-start(bf16[256,128]{1,0:T(8,128)(2,1)} %copy-done.6) | copy-start | bytes 196612
  221.2 25.5 %collective-permute-start.12 = (f32[128,4096]{1,0:T(8,128)S(1)}, f32[128,4096]{1,0:T(8,128)S(1)}, u32[]{:S(2)}, u32[]{:S(2)}) collective-permute-start(f32[128,4096]{1,0:T(8,128)S(1)} %add.92), channel_id=1, source_target_pairs={{1,0},{2,1},{3,2},{4,3},{5,4},{6,5},{7,6},{8,7},{9,8},{10,9},{11,1... | collective-permute-start | bytes 6291464 | tf_op jit(solution)/shard_map/ppermute | solution.py:22
  224.6 27.7 %copy-start.5 = (bf16[256,128]{1,0:T(8,128)(2,1)S(1)}, bf16[256,128]{1,0:T(8,128)(2,1)}, u32[]{:S(2)}) copy-start(bf16[256,128]{1,0:T(8,128)(2,1)} %copy-done.4) | copy-start | bytes 196612
  247.0 25.5 %collective-permute-start.13 = (f32[128,4096]{1,0:T(8,128)S(1)}, f32[128,4096]{1,0:T(8,128)S(1)}, u32[]{:S(2)}, u32[]{:S(2)}) collective-permute-start(f32[128,4096]{1,0:T(8,128)S(1)} %add.93), channel_id=1, source_target_pairs={{1,0},{2,1},{3,2},{4,3},{5,4},{6,5},{7,6},{8,7},{9,8},{10,9},{11,1... | collective-permute-start | bytes 6291464 | tf_op jit(solution)/shard_map/ppermute | solution.py:22
  272.8 78.0 %collective-permute-start.14 = (f32[128,4096]{1,0:T(8,128)S(1)}, f32[128,4096]{1,0:T(8,128)}, u32[]{:S(2)}, u32[]{:S(2)}) collective-permute-start(f32[128,4096]{1,0:T(8,128)S(1)} %add.94), channel_id=1, source_target_pairs={{25,0},{26,1},{27,2},{28,3},{29,4},{30,5},{31,6},{0,7},{1,8},{2,9}... | collective-permute-start | bytes 6291464 | tf_op jit(solution)/shard_map/ppermute | solution.py:22
  746.2 3.2 copy-start
Sparse Core Ops, SparseCore 0:
  204.2 536.9 all-gather.2
Sparse Core Ops, SparseCore 1:
  351.0 132.9 all-reduce.1
